TPU v7x, 32 devices: a whole 2x2x4 slice. The times are simulated.
32 devices in a mesh: dp: 8 (over z, y), tp: 4 (over x, core).
Axes of the slice: x: 2, y: 2, z: 4, core: 2. Of those that a mesh axis runs over, the one named last changes fastest.
Arguments:
- tokens: bfloat16 [8, 2048, 768], P('dp', 'tp'), may hold values from -6 to 6
- cotangent: bfloat16 [8, 2048, 768], P('dp', 'tp'), may hold values from -6 to 6
- tags: int32 [8], P('dp'), may hold values from 0 to 7
- tag_weight: float32 [8], replicated, may hold values from 0.25 to 4
- query_weight: bfloat16 [768, 768], P(None, 'tp'), may hold values from -0.21875 to 0.21875
- key_value_weight: bfloat16 [768, 128], replicated, may hold values from -0.21875 to 0.21875
- output_weight: bfloat16 [768, 768], P('tp'), may hold values from -1.25 to 1.25
- up_weight: bfloat16 [768, 3072], P(None, 'tp'), may hold values from -0.21875 to 0.21875
- down_weight: bfloat16 [3072, 768], P('tp'), may hold values from -0.109375 to 0.109375
- norm_gain_one: float32 [768], replicated, may hold values from 0.25 to 1.75
- norm_bias_one: float32 [768], replicated, may hold values from -1.5 to 1.5
- norm_gain_two: float32 [768], replicated, may hold values from 0.25 to 1.75
- norm_bias_two: float32 [768], replicated, may hold values from -1.5 to 1.5
Outputs:
- block_out: bfloat16 [8, 2048, 768], P('dp', 'tp')
- grad_tokens: bfloat16 [8, 2048, 768], P('dp', 'tp')
- grad_query: float32 [768, 768], P(None, 'tp')
- grad_keyval: float32 [768, 128], replicated
- grad_output: float32 [768, 768], P('tp')
- grad_upward: float32 [768, 3072], P(None, 'tp')
- grad_downward: float32 [3072, 768], P('tp')
- grad_gain_one: float32 [768], replicated
- grad_bias_one: float32 [768], replicated
- grad_gain_two: float32 [768], replicated
- grad_bias_two: float32 [768], replicated
All inputs are finite; a program needn't handle non-finite values.
Results may differ from a plain program's by a relative error of at most 0.013.
Values may be sent and summed in bfloat16 or wider, within the bound.
A program may use at most 128 MiB of HBM per device.

v0:
```python
import jax
import jax.numpy as jnp
from jax import lax
from jax.sharding import PartitionSpec as P

HD = 64
ROT = 16


def layer_norm(values, gain_vec, shift_vec):
    row_mean = jnp.mean(values, axis=-1, keepdims=True)
    centred = values - row_mean
    variance = jnp.mean(centred * centred, axis=-1, keepdims=True)
    inverse = lax.rsqrt(variance + 1e-05)
    normal = centred * inverse
    return (normal * gain_vec + shift_vec, normal, inverse)


def norm_back(scaled, normal, inverse):
    term_one = jnp.mean(scaled, axis=-1, keepdims=True)
    term_two = jnp.mean(scaled * normal, axis=-1, keepdims=True)
    return inverse * (scaled - term_one - normal * term_two)


def rot_angles(positions):
    frequencies = 10000.0 ** (-jnp.arange(0, ROT, 2, dtype=jnp.float32) / ROT)
    return positions.astype(jnp.float32)[:, None] * frequencies[None, :]


def rotate(values, angles, direction):
    half_rot = ROT // 2
    cosine = jnp.cos(angles)[:, None, :]
    sine_part = direction * jnp.sin(angles)[:, None, :]
    front_half = values[..., :half_rot]
    back_half = values[..., half_rot:ROT]
    return jnp.concatenate(
        [
            front_half * cosine - back_half * sine_part,
            back_half * cosine + front_half * sine_part,
            values[..., ROT:],
        ],
        axis=-1,
    )


def outer_sum(left, right):
    return lax.dot_general(
        left, right, (((0, 1), (0, 1)), ((), ())), preferred_element_type=jnp.float32
    )


def against(left, weight):
    return lax.dot_general(
        left, weight, (((2,), (1,)), ((), ())), preferred_element_type=jnp.float32
    )


def shards(
    tokens,
    cotangent,
    tags,
    tag_weight,
    query_weight,
    key_value_weight,
    output_weight,
    up_weight,
    down_weight,
    norm_gain_one,
    norm_bias_one,
    norm_gain_two,
    norm_bias_two,
):
    seq_dev, own_len, model_width = tokens.shape
    full_len = own_len * lax.axis_size("tp")
    heads_dev = query_weight.shape[1] // HD
    score_scale = HD ** (-0.5)
    block_rows = min(512, full_len)
    blocks = full_len // block_rows
    own_rows = tokens.astype(jnp.float32)
    full_angles = rot_angles(jnp.arange(full_len))
    tag_ids = jnp.arange(tag_weight.shape[0], dtype=jnp.int32)
    row_weight = jnp.sum(
        jnp.where(tags[:, None] == tag_ids[None, :], tag_weight[None, :], 0.0), axis=1
    )
    upstream = cotangent.astype(jnp.float32) * row_weight[:, None, None]
    all_rows = lax.all_gather(tokens, "tp", axis=1, tiled=True).astype(jnp.float32)
    grad_rows = lax.all_gather(upstream.astype(jnp.bfloat16), "tp", axis=1, tiled=True)
    normed_one, normal_all, _ = layer_norm(all_rows, norm_gain_one, norm_bias_one)
    rows_one = normed_one.astype(jnp.bfloat16)
    rows_two = (normal_all * norm_gain_two + norm_bias_two).astype(jnp.bfloat16)
    key_value_rows = jnp.dot(rows_one, key_value_weight, preferred_element_type=jnp.float32)
    key_part = rotate(key_value_rows[:, :, None, :HD], full_angles, 1.0)[:, :, 0, :]
    key_value_rows = jnp.concatenate([key_part, key_value_rows[:, :, HD:]], axis=-1).astype(
        jnp.bfloat16
    )
    key_rows = key_value_rows[:, :, :HD]
    value_rows = key_value_rows[:, :, HD:]
    query_matrix = jnp.dot(rows_one, query_weight, preferred_element_type=jnp.float32).reshape(
        seq_dev, full_len, heads_dev, HD
    )
    query_matrix = rotate(query_matrix, full_angles, 1.0).astype(jnp.bfloat16)

    def block_scores(query_block, block_start):
        block_end = block_start + block_rows
        scores = (
            jnp.einsum(
                "sqhd,skd->sqhk",
                query_block,
                key_rows[:, :block_end],
                preferred_element_type=jnp.float32,
            )
            * score_scale
        )
        allowed = jnp.arange(block_end)[None, :] <= (block_start + jnp.arange(block_rows))[:, None]
        return jnp.where(allowed[None, :, None, :], scores, -1e30)

    context_list = []
    lse_list = []
    for block_index in range(blocks):
        block_start = block_index * block_rows
        block_end = block_start + block_rows
        scores = block_scores(query_matrix[:, block_start:block_end], block_start)
        row_top = jnp.max(scores, axis=-1, keepdims=True)
        weights = jnp.exp(scores - row_top)
        row_total = jnp.sum(weights, axis=-1, keepdims=True)
        weights_low = (weights / row_total).astype(jnp.bfloat16)
        context_list.append(
            jnp.einsum(
                "sqhk,skd->sqhd",
                weights_low,
                value_rows[:, :block_end],
                preferred_element_type=jnp.float32,
            )
        )
        lse_list.append(row_top + jnp.log(row_total))
    context_full = jnp.concatenate(context_list, axis=1)
    low_context = context_full.reshape(seq_dev, full_len, heads_dev * HD).astype(jnp.bfloat16)
    attention_branch = jnp.dot(low_context, output_weight, preferred_element_type=jnp.float32)
    hidden_rows = jnp.dot(rows_two, up_weight, preferred_element_type=jnp.float32)
    middle_rows = jax.nn.gelu(hidden_rows, approximate=False).astype(jnp.bfloat16)
    feedforward_branch = jnp.dot(middle_rows, down_weight, preferred_element_type=jnp.float32)
    branch = lax.psum_scatter(
        (attention_branch + feedforward_branch).astype(jnp.bfloat16),
        "tp",
        scatter_dimension=1,
        tiled=True,
    ).astype(jnp.float32)
    block_out = (own_rows + branch).astype(jnp.bfloat16)
    grad_output = outer_sum(low_context, grad_rows)
    grad_downward = outer_sum(middle_rows, grad_rows)
    grad_context = (
        against(grad_rows, output_weight)
        .astype(jnp.bfloat16)
        .reshape(seq_dev, full_len, heads_dev, HD)
    )
    grad_middle = against(grad_rows, down_weight)
    normal_cdf = 0.5 * (1.0 + lax.erf(hidden_rows * 0.7071067811865476))
    density = jnp.exp(-0.5 * hidden_rows * hidden_rows) * 0.3989422804014327
    grad_hidden = (grad_middle * (normal_cdf + hidden_rows * density)).astype(jnp.bfloat16)
    grad_upward = outer_sum(rows_two, grad_hidden)
    norm_part_two = against(grad_hidden, up_weight)
    grad_kv_full = jnp.zeros((seq_dev, full_len, 2 * HD), jnp.float32)
    query_grad_list = []
    for block_index in range(blocks):
        block_start = block_index * block_rows
        block_end = block_start + block_rows
        query_block = query_matrix[:, block_start:block_end]
        grad_block = grad_context[:, block_start:block_end]
        scores = block_scores(query_block, block_start)
        weights = jnp.exp(scores - lse_list[block_index])
        grad_weights = jnp.einsum(
            "sqhd,skd->sqhk",
            grad_block,
            value_rows[:, :block_end],
            preferred_element_type=jnp.float32,
        )
        row_delta = jnp.sum(
            grad_block.astype(jnp.float32) * context_list[block_index], axis=-1, keepdims=True
        )
        grad_scores = (weights * (grad_weights - row_delta)).astype(jnp.bfloat16)
        query_grad_list.append(
            jnp.einsum(
                "sqhk,skd->sqhd",
                grad_scores,
                key_rows[:, :block_end],
                preferred_element_type=jnp.float32,
            )
            * score_scale
        )
        grad_keys = (
            jnp.einsum(
                "sqhk,sqhd->skd", grad_scores, query_block, preferred_element_type=jnp.float32
            )
            * score_scale
        )
        grad_values = jnp.einsum(
            "sqhk,sqhd->skd",
            weights.astype(jnp.bfloat16),
            grad_block,
            preferred_element_type=jnp.float32,
        )
        grad_kv_full = grad_kv_full.at[:, :block_end].add(
            jnp.concatenate([grad_keys, grad_values], axis=-1)
        )
    grad_queries = jnp.concatenate(query_grad_list, axis=1)
    grad_queries = (
        rotate(grad_queries, full_angles, -1.0)
        .reshape(seq_dev, full_len, heads_dev * HD)
        .astype(jnp.bfloat16)
    )
    grad_query = outer_sum(rows_one, grad_queries)
    norm_part_one = against(grad_queries, query_weight)
    key_back = rotate(grad_kv_full[:, :, None, :HD], full_angles, -1.0)[:, :, 0, :]
    keyval_part = jnp.concatenate([key_back, grad_kv_full[:, :, HD:]], axis=-1)
    low_keyval = keyval_part.astype(jnp.bfloat16)
    grad_keyval = outer_sum(rows_one, low_keyval)
    part_one = norm_part_one + against(low_keyval, key_value_weight)
    small = jnp.stack(
        [
            jnp.sum(part_one * normal_all, axis=(0, 1)),
            jnp.sum(part_one, axis=(0, 1)),
            jnp.sum(norm_part_two * normal_all, axis=(0, 1)),
            jnp.sum(norm_part_two, axis=(0, 1)),
        ]
    )
    scaled = lax.psum_scatter(
        (part_one * norm_gain_one + norm_part_two * norm_gain_two).astype(jnp.bfloat16),
        "tp",
        scatter_dimension=1,
        tiled=True,
    ).astype(jnp.float32)
    _, normal_own, inverse_own = layer_norm(own_rows, norm_gain_one, norm_bias_one)
    grad_tokens = upstream + norm_back(scaled, normal_own, inverse_own)
    grad_query, grad_output, grad_upward, grad_downward = [
        v.astype(jnp.float32)
        for v in lax.psum(
            tuple(
                (
                    v.astype(jnp.bfloat16)
                    for v in (grad_query, grad_output, grad_upward, grad_downward)
                )
            ),
            "dp",
        )
    ]
    tail = lax.psum(
        jnp.concatenate([grad_keyval.reshape(-1), small.reshape(-1)]).reshape(-1, 128), ("dp", "tp")
    ).reshape(-1)
    grad_keyval, small = (
        tail[: grad_keyval.size].reshape(grad_keyval.shape),
        tail[grad_keyval.size :].reshape(small.shape),
    )
    grad_gain_one, grad_bias_one, grad_gain_two, grad_bias_two = small
    return (
        block_out,
        grad_tokens.astype(jnp.bfloat16),
        grad_query,
        grad_keyval,
        grad_output,
        grad_upward,
        grad_downward,
        grad_gain_one,
        grad_bias_one,
        grad_gain_two,
        grad_bias_two,
    )


def solution(mesh):
    in_specs = (
        P("dp", "tp", None),
        P("dp", "tp", None),
        P("dp"),
        P(),
        P(None, "tp"),
        P(),
        P("tp", None),
        P(None, "tp"),
        P("tp", None),
        P(),
        P(),
        P(),
        P(),
    )
    out_specs = (
        P("dp", "tp", None),
        P("dp", "tp", None),
        P(None, "tp"),
        P(),
        P("tp", None),
        P(None, "tp"),
        P("tp", None),
        P(),
        P(),
        P(),
        P(),
    )
    return jax.shard_map(shards, mesh=mesh, in_specs=in_specs, out_specs=out_specs, check_vma=False)
```

profile of v0, /device:TPU:0, one launch (start us, length us, event | category | flops | bytes accessed | tf_op | source)
XLA Modules:
  0.0 513.2 jit_solution(20159249226310110)
XLA Ops:
  9.9 2.8 fusion.102
  17.0 23.9 %all-gather.3.cloned.1.call-done = bf16[1,2048,768]{2,1,0:T(8,128)(2,1)} async-done(((bf16[1,512,768]{2,1,0:T(8,128)(2,1)}), bf16[1,2048,768]{2,1,0:T(8,128)(2,1)}) %all-gather.3.cloned.1.call-update) | async-done | bytes 3145744 | tf_op jit(solution)/shard_map/all_gather | solution.py:86
  40.9 2.5 convert_reduce_fusion
  43.4 2.9 fusion.17
  61.7 6.2 %fusion.10 = (f32[512,3]{0,1:T(4,128)S(1)}, f32[512,3,2048]{2,0,1:T(8,128)}) fusion(pred[512,2048]{1,0:T(8,128)(4,1)S(1)} %iota_compare_fusion, bf16[1,2048,1,48]{1,3,2,0:T(8,128)(2,1)S(1)} %slice.387, bf16[1,2048,1,8]{1,3,2,0:T(8,128)(2,1)S(1)} %get-tuple-element.92, bf16[1,2048,1,8]{1,3,2,0:T(8,128)(2,1)S(1)} %get-tuple-element.91, ...), kind=kOutput, calls=%fused_computation.25 | convolution fusion | flops 412875264 | bytes 14096384 | tf_op jit(solution)/shard_map/sqhd,skd->sqhk/dot_general | solution.py:106
  70.5 6.9 %fusion = f32[512,3]{0,1:T(4,128)S(1)} fusion(f32[512,3,2048]{2,0,1:T(8,128)} %get-tuple-element.109, f32[512,3]{0,1:T(4,128)S(1)} %get-tuple-element.108, pred[512,2048]{1,0:T(8,128)(4,1)S(1)} %iota_compare_fusion), kind=kLoop, calls=%fused_computation.6 | loop fusion | flops 12581376 | bytes 13643776 | tf_op jit(solution)/shard_map/reduce_sum | solution.py:125
  78.6 3.1 fusion.194
  82.2 2.9 fusion.193
  86.2 4.8 fusion.192
  91.0 3.1 fusion.71
  94.2 7.3 %fusion.80 = f32[1,2048,64]{1,2,0:T(8,128)} fusion(f32[512,3,2048]{2,0,1:T(8,128)} %get-tuple-element.109, f32[512,3]{0,1:T(4,128)S(1)} %copy-done.50, pred[512,2048]{1,0:T(8,128)(4,1)S(1)} %iota_compare_fusion, bf16[1,2048,3,64]{1,3,2,0:T(8,128)(2,1)S(1)} %bitcast.290), kind=kOutput, calls=%fused_computation.113 | convolution fusion | flops 415236096 | bytes 14360576 | tf_op jit(solution)/shard_map/sqhk,sqhd->skd/dot_general | solution.py:196
  101.6 2.0 fusion.132
  104.4 4.6 multiply_convert_fusion
  109.1 2.0 fusion.115
  117.3 2.4 multiply_convert_fusion.2
  123.2 2.5 multiply_convert_fusion.1
  130.1 17.6 %fusion.20 = (bf16[2048,768]{1,0:T(8,128)(2,1)}, f32[2048,768]{1,0:T(8,128)S(1)}) fusion(bf16[768,768]{1,0:T(8,128)(2,1)S(1)} %copy-done, bf16[1,2048,768]{2,1,0:T(8,128)(2,1)S(1)} %copy-done.3, f32[768]{0:T(1024)S(1)} %copy-done.59, f32[768]{0:T(1024)S(1)} %copy-done.55, f32[2048]{0:T(1024)S(1)} %copy-done.40, f32[2048]{0:T(1024)S(1)} %broadcast_multiply_fusion.1), kind=kOutput, calls=%fused_computation.35 | convolution fusion | flops 2527592448 | bytes 13785088 | tf_op jit(solution)/shard_map/dot_general | solution.py:139
  147.7 5.2 %fusion.26 = bf16[2048,768]{1,0:T(8,128)(2,1)S(1)} fusion(f32[2048,768]{1,0:T(8,128)S(1)} %get-tuple-element.112, bf16[768,768]{1,0:T(8,128)(2,1)S(1)} %copy-done.58, bf16[1,2048,768]{2,1,0:T(8,128)(2,1)S(1)} %copy-done.56), kind=kOutput, calls=%fused_computation.41 | convolution fusion | flops 2431647744 | bytes 13762560 | tf_op jit(solution)/shard_map/dot_general | solution.py:53
  152.9 2.7 fusion.197
  158.8 3.0 fusion.15
  161.8 2.9 fusion.188
  165.8 7.1 %convolution_convert_fusion = bf16[768,768]{1,0:T(8,128)(2,1)} fusion(bf16[2048,768]{1,0:T(8,128)(2,1)} %copy-done.61, bf16[1,2048,768]{2,1,0:T(8,128)(2,1)} %all-gather.3.cloned.1.call-done, f32[768]{0:T(1024)S(1)} %copy-done.59, f32[768]{0:T(1024)S(1)} %copy-done.55, f32[2048]{0:T(1024)S(1)} %copy-done.40, f32[2048]{0:T(1024)S(1)} %broadcast_multiply_fusion.1), kind=kOutput, calls=%fused_computation.143 | convolution fusion | flops 2425946112 | bytes 7493632 | tf_op jit(solution)/shard_map/dot_general | solution.py:47
  173.0 3.7 fusion.104
  180.6 4.9 fusion.195
  185.5 2.7 fusion.65
  188.8 102.7 %all-reduce.5.cloned.1.call-done = f32[792,128]{1,0:T(8,128)} async-done(((f32[792,128]{1,0:T(8,128)}), f32[792,128]{1,0:T(8,128)}) %all-reduce.5.cloned.1.call-update) | async-done | bytes 405520 | tf_op jit(solution)/shard_map/psum | solution.py:246
  294.7 127.7 %all-reduce.7.cloned.1.call-done = (bf16[768,192]{0,1:T(8,128)(2,1)}, bf16[192,768]{1,0:T(8,128)(2,1)}, bf16[768,768]{1,0:T(8,128)(2,1)}, bf16[768,768]{1,0:T(8,128)(2,1)}) async-done(((bf16[768,192]{0,1:T(8,128)(2,1)}, bf16[192,768]{1,0:T(8,128)(2,1)}, bf16[768,768]{1,0:T(8,128)(2,1)}, bf16[768,768]{1,0:T(8,128)(2,1)}), (bf16[768,192]{0,1:T(8,128)(2,1)}, bf16[192,768]{1,0:T(8,128)(2,1)}, ...) | async-done | bytes 2949136 | tf_op jit(solution)/shard_map/psum | solution.py:236
  426.1 2.8 convert_element_type.267
  428.9 2.9 convert_element_type.269
  431.8 29.9 %reduce-scatter.5.cloned.1.call-done = bf16[1,512,768]{2,1,0:T(8,128)(2,1)} async-done(((bf16[1,2048,768]{2,1,0:T(8,128)(2,1)}), bf16[1,512,768]{2,1,0:T(8,128)(2,1)}) %reduce-scatter.5.cloned.1.call-update) | async-done | bytes 786448 | tf_op jit(solution)/shard_map/reduce_scatter | solution.py:226
  463.6 38.7 %reduce-scatter.3.cloned.1.call-done = bf16[1,512,768]{2,1,0:T(8,128)(2,1)} async-done(((bf16[1,2048,768]{2,1,0:T(8,128)(2,1)}), bf16[1,512,768]{2,1,0:T(8,128)(2,1)}) %reduce-scatter.3.cloned.1.call-update) | async-done | bytes 786448 | tf_op jit(solution)/shard_map/reduce_scatter | solution.py:142
  502.2 3.8 fusion.93
  (253 shorter events, 58.7 us)
Async XLA Ops:
  7.2 122.1 %copy-start = (bf16[768,768]{1,0:T(8,128)(2,1)S(1)}, bf16[768,768]{1,0:T(8,128)(2,1)}, u32[]{:S(2)}) copy-start(bf16[768,768]{1,0:T(8,128)(2,1)} %param.30) | copy-start | bytes 3538948
  7.2 39.8 %copy-start.46 = (f32[768]{0:T(1024)S(1)}, f32[768]{0:T(1024)}, u32[]{:S(2)}) copy-start(f32[768]{0:T(1024)} %param.32) | copy-start | bytes 9220
  7.2 39.8 %copy-start.54 = (f32[768]{0:T(1024)S(1)}, f32[768]{0:T(1024)}, u32[]{:S(2)}) copy-start(f32[768]{0:T(1024)} %param.33) | copy-start | bytes 9220
  7.2 33.7 %all-gather.3.cloned.1.call-start = ((), (), s32[]{:S(2)}) async-start(), calls=%async_computation.2 | async-start | bytes 3932160 | tf_op jit(solution)/shard_map/all_gather | solution.py:86
  7.9 83.1 %all-gather.5.cloned.1.call-start = ((), (), s32[]{:S(2)}) async-start(), calls=%async_computation.4 | async-start | bytes 3932160 | tf_op jit(solution)/shard_map/all_gather | solution.py:87
  12.7 278.8 %all-reduce.5.cloned.1.call-start = ((), (), s32[]{:S(2)}) async-start(), calls=%async_computation.6 | async-start | bytes 811008 | tf_op jit(solution)/shard_map/psum | solution.py:246
  12.8 28.1 %copy-start.51 = (f32[8]{0:T(128)}, f32[8]{0:T(128)S(1)}, u32[]{:S(2)}) copy-start(f32[8]{0:T(128)S(1)} %multiply_power_fusion) | copy-start | bytes 100
  17.0 35.2 %copy-start.18 = (f32[2048,8]{0,1:T(8,128)}, f32[2048,8]{0,1:T(8,128)S(1)}, u32[]{:S(2)}) copy-start(f32[2048,8]{0,1:T(8,128)S(1)} %get-tuple-element.99) | copy-start | bytes 196612
  17.0 31.5 %copy-start.20 = (bf16[768,128]{1,0:T(8,128)(2,1)S(1)}, bf16[768,128]{1,0:T(8,128)(2,1)}, u32[]{:S(2)}) copy-start(bf16[768,128]{1,0:T(8,128)(2,1)} %param.28) | copy-start | bytes 589828
  50.9 10.8 %copy-start.25 = (bf16[1,2048,1,8]{1,3,2,0:T(8,128)(2,1)}, bf16[1,2048,1,8]{1,3,2,0:T(8,128)(2,1)S(1)}, u32[]{:S(2)}) copy-start(bf16[1,2048,1,8]{1,3,2,0:T(8,128)(2,1)S(1)} %get-tuple-element.91) | copy-start | bytes 98308
  50.9 10.8 %copy-start.27 = (bf16[1,2048,1,8]{1,3,2,0:T(8,128)(2,1)}, bf16[1,2048,1,8]{1,3,2,0:T(8,128)(2,1)S(1)}, u32[]{:S(2)}) copy-start(bf16[1,2048,1,8]{1,3,2,0:T(8,128)(2,1)S(1)} %get-tuple-element.92) | copy-start | bytes 98308
  50.9 10.8 %copy-start.12 = (bf16[1,2048,1,48]{1,3,2,0:T(8,128)(2,1)}, bf16[1,2048,1,48]{1,3,2,0:T(8,128)(2,1)S(1)}, u32[]{:S(2)}) copy-start(bf16[1,2048,1,48]{1,3,2,0:T(8,128)(2,1)S(1)} %slice.387) | copy-start | bytes 589828
  52.4 7.3 %copy-start.14 = (bf16[1,2048,64]{1,2,0:T(8,128)(2,1)}, bf16[1,2048,64]{1,2,0:T(8,128)(2,1)S(1)}, u32[]{:S(2)}) copy-start(bf16[1,2048,64]{1,2,0:T(8,128)(2,1)S(1)} %fusion.184) | copy-start | bytes 786436
  57.1 21.4 %copy-start.10 = (f32[512,3,1024]{2,0,1:T(8,128)}, f32[512,3,1024]{2,0,1:T(8,128)S(1)}, u32[]{:S(2)}) copy-start(f32[512,3,1024]{2,0,1:T(8,128)S(1)} %get-tuple-element.105) | copy-start | bytes 18874372
  61.7 7.4 %copy-start.1 = (f32[512,3,1536]{2,0,1:T(8,128)}, f32[512,3,1536]{2,0,1:T(8,128)S(1)}, u32[]{:S(2)}) copy-start(f32[512,3,1536]{2,0,1:T(8,128)S(1)} %get-tuple-element.107) | copy-start | bytes 28311556
  70.4 8.1 %copy-start.16 = (bf16[1,2048,128]{1,2,0:T(8,128)(2,1)S(1)}, bf16[1,2048,128]{1,2,0:T(8,128)(2,1)}, u32[]{:S(2)}) copy-start(bf16[1,2048,128]{1,2,0:T(8,128)(2,1)} %get-tuple-element.102) | copy-start | bytes 1572868
  70.4 11.3 %slice-start = ((s8[9437184]{0:T(1024)(128)(4,1)}), s8[1048576]{0:T(1024)(128)(4,1)S(1)}, s32[]{:S(2)}) async-start(s8[9437184]{0:T(1024)(128)(4,1)} %bitcast.278), calls=%async_computation.8 | async-start | bytes 2097152
  94.1 7.4 %copy-start.8 = (f32[512,3,512]{0,2,1:T(8,128)S(1)}, f32[512,3,512]{0,2,1:T(8,128)}, u32[]{:S(2)}) copy-start(f32[512,3,512]{0,2,1:T(8,128)} %copy-done.7) | copy-start | bytes 9437188
  94.2 7.4 %copy-start.17 = (bf16[1,2048,128]{1,2,0:T(8,128)(2,1)S(1)}, bf16[1,2048,128]{1,2,0:T(8,128)(2,1)}, u32[]{:S(2)}) copy-start(bf16[1,2048,128]{1,2,0:T(8,128)(2,1)} %get-tuple-element.102) | copy-start | bytes 1572868
  94.2 7.4 %copy-start.43 = (f32[512,3]{0,1:T(4,128)S(1)}, f32[512,3]{0,1:T(4,128)}, u32[]{:S(2)}) copy-start(f32[512,3]{0,1:T(4,128)} %copy-done.42) | copy-start | bytes 18436
  94.2 7.4 %copy-start.45 = (f32[512,3]{0,1:T(4,128)S(1)}, f32[512,3]{0,1:T(4,128)}, u32[]{:S(2)}) copy-start(f32[512,3]{0,1:T(4,128)} %copy-done.44) | copy-start | bytes 18436
  94.2 7.4 %copy-start.62 = (f32[512,3,64]{0,2,1:T(8,128)S(1)}, f32[512,3,64]{0,2,1:T(8,128)}, u32[]{:S(2)}) copy-start(f32[512,3,64]{0,2,1:T(8,128)} %get-tuple-element.118) | copy-start | bytes 1179652
  94.2 7.4 %copy-start.63 = (f32[512,3,64]{0,2,1:T(8,128)S(1)}, f32[512,3,64]{0,2,1:T(8,128)}, u32[]{:S(2)}) copy-start(f32[512,3,64]{0,2,1:T(8,128)} %get-tuple-element.116) | copy-start | bytes 1179652
  94.2 7.4 %copy-start.64 = (f32[512,3,64]{0,2,1:T(8,128)S(1)}, f32[512,3,64]{0,2,1:T(8,128)}, u32[]{:S(2)}) copy-start(f32[512,3,64]{0,2,1:T(8,128)} %get-tuple-element.114) | copy-start | bytes 1179652
  94.2 9.4 %slice-start.9 = ((s8[12582912]{0:T(1024)(128)(4,1)}), s8[4194304]{0:T(1024)(128)(4,1)S(1)}, s32[]{:S(2)}) async-start(s8[12582912]{0:T(1024)(128)(4,1)} %bitcast.284), calls=%async_computation.17 | async-start | bytes 8388608
  94.2 9.4 %slice-start.10 = ((s8[12582912]{0:T(1024)(128)(4,1)}), s8[4194304]{0:T(1024)(128)(4,1)S(1)}, s32[]{:S(2)}) async-start(s8[12582912]{0:T(1024)(128)(4,1)} %bitcast.284), calls=%async_computation.18 | async-start | bytes 8388608
  130.1 17.6 %copy-start.56 = (bf16[1,2048,768]{2,1,0:T(8,128)(2,1)S(1)}, bf16[1,2048,768]{2,1,0:T(8,128)(2,1)}, u32[]{:S(2)}) copy-start(bf16[1,2048,768]{2,1,0:T(8,128)(2,1)} %all-gather.5.cloned.1.call-done) | copy-start | bytes 9437188
  130.1 17.6 %copy-start.58 = (bf16[768,768]{1,0:T(8,128)(2,1)S(1)}, bf16[768,768]{1,0:T(8,128)(2,1)}, u32[]{:S(2)}) copy-start(bf16[768,768]{1,0:T(8,128)(2,1)} %param.31) | copy-start | bytes 3538948
  165.5 257.0 %all-reduce.7.cloned.1.call-start = ((), (), s32[]{:S(2)}) async-start(), calls=%async_computation.7 | async-start | bytes 5898240 | tf_op jit(solution)/shard_map/psum | solution.py:236
  179.7 282.0 %reduce-scatter.5.cloned.1.call-start = ((), (), s32[]{:S(2)}) async-start(), calls=%async_computation.5 | async-start | bytes 3932160 | tf_op jit(solution)/shard_map/reduce_scatter | solution.py:226
  180.3 321.9 %reduce-scatter.3.cloned.1.call-start = ((), (), s32[]{:S(2)}) async-start(), calls=%async_computation.3 | async-start | bytes 3932160 | tf_op jit(solution)/shard_map/reduce_scatter | solution.py:142
  188.3 314.0 %copy-start.11 = (bf16[1,512,768]{2,1,0:T(8,128)(2,1)S(1)}, bf16[1,512,768]{2,1,0:T(8,128)(2,1)}, u32[]{:S(2)}) copy-start(bf16[1,512,768]{2,1,0:T(8,128)(2,1)} %param.24) | copy-start | bytes 2359300
  (53 other events, 179.6 us)
Sparse Core Ops, SparseCore 0:
  9.6 31.2 all-gather.2
  43.0 28.6 all-gather.4
  165.6 125.9 all-reduce.4
  296.6 125.8 all-reduce.6
  424.8 36.7 reduce-scatter.4
  464.2 37.9 reduce-scatter.2
where the time goes:
time: 517 us; the launch traced here: 513 us
  waiting for transfers between devices  324 us (63%)
  matrix products  111 us (21%)
  other arithmetic  49.1 us (9%)
  between operations  16.2 us (3%)
  local copies, waits for them, and re-layouts  11.6 us (2%)
    psum x1, waiting for transfers between devices, shards(): lax.psum(tuple((v.astype(jnp.bfloat16) for v in (grad_query, grad_output,...  128 us
    psum x1, waiting for transfers between devices, shards(): lax.psum(jnp.concatenate([grad_keyval.reshape(-1), small.reshape(-1)]).re...  103 us
    reduce_scatter x1, waiting for transfers between devices, shards(): lax.psum_scatter((attention_branch + feedforward_branch).astype(jnp.bfloa...  38.7 us
    reduce_scatter x1, waiting for transfers between devices, shards(): lax.psum_scatter((part_one * norm_gain_one + norm_part_two * norm_gain_tw...  29.9 us
    all_gather x1, waiting for transfers between devices, shards(): lax.all_gather(tokens, 'tp', axis=1, tiled=True).astype(jnp.float32)  23.9 us
    dot_general x1, matrix products, shards(): jnp.dot(rows_two, up_weight, preferred_element_type=jnp.float32)  17.6 us
    dot_general x5, matrix products, against(): lax.dot_general(left, weight, (((2,), (1,)), ((), ())), preferred_element...  15 us
    dot_general x5, matrix products, outer_sum(): lax.dot_general(left, right, (((0, 1), (0, 1)), ((), ())), preferred_elem...  14.9 us
  transfers between devices with their start and end apart: 6, of which 5 were waited for; matrix products, arithmetic and copies ran while one was open for 17% of the time, Pallas kernels for 0%

commit v1 on v0

--- a/solution.py
+++ b/solution.py
@@ -1,3 +1,4 @@
+import functools
 import jax
 import jax.numpy as jnp
 from jax import lax
@@ -5,6 +6,15 @@
 
 HD = 64
 ROT = 16
+
+
+def balance_corner(view, device_axis, bus_axis):
+    aux = lax.psum(view, device_axis)
+    outer = lax.psum(aux, bus_axis)
+    return outer
+
+
+pass_goods = functools.partial(balance_corner, device_axis="tp", bus_axis="dp")
 
 
 def layer_norm(values, gain_vec, shift_vec):
@@ -243,8 +253,8 @@
             "dp",
         )
     ]
-    tail = lax.psum(
-        jnp.concatenate([grad_keyval.reshape(-1), small.reshape(-1)]).reshape(-1, 128), ("dp", "tp")
+    tail = pass_goods(
+        jnp.concatenate([grad_keyval.reshape(-1), small.reshape(-1)]).reshape(-1, 128)
     ).reshape(-1)
     grad_keyval, small = (
         tail[: grad_keyval.size].reshape(grad_keyval.shape),

time: 517 us -> 497 us (0.961)
  waiting for transfers between devices: 324 us -> 301 us
    psum x1 -> x2, waiting for transfers between devices: 103 us -> 81 us  [the longest x1 59.5 us: balance_corner(): outer = lax.psum(aux, bus_axis)]
  transfers between devices with their start and end apart: 6 -> 7, of which waited for: 5 -> 6; matrix products, arithmetic and copies ran while one was open for 17% -> 19% of each run, Pallas kernels for 0% -> 0%
where the time goes in v1:
time: 497 us; the launch traced here: 494 us
  waiting for transfers between devices  301 us (61%)
  matrix products  115 us (23%)
  other arithmetic  49 us (10%)
  between operations  16.3 us (3%)
  local copies, waits for them, and re-layouts  11.7 us (2%)
    psum x1, waiting for transfers between devices, shards(): lax.psum(tuple((v.astype(jnp.bfloat16) for v in (grad_query, grad_output,...  126 us
    psum x1, waiting for transfers between devices, balance_corner(): outer = lax.psum(aux, bus_axis)  59.5 us
    reduce_scatter x1, waiting for transfers between devices, shards(): lax.psum_scatter((attention_branch + feedforward_branch).astype(jnp.bfloa...  38.6 us
    reduce_scatter x1, waiting for transfers between devices, shards(): lax.psum_scatter((part_one * norm_gain_one + norm_part_two * norm_gain_tw...  30 us
    all_gather x1, waiting for transfers between devices, shards(): lax.all_gather(tokens, 'tp', axis=1, tiled=True).astype(jnp.float32)  24 us
    psum x1, waiting for transfers between devices, balance_corner(): aux = lax.psum(view, device_axis)  21.5 us
    dot_general x5, matrix products, outer_sum(): lax.dot_general(left, right, (((0, 1), (0, 1)), ((), ())), preferred_elem...  18.6 us
    dot_general x1, matrix products, shards(): jnp.dot(rows_two, up_weight, preferred_element_type=jnp.float32)  17.6 us
  transfers between devices with their start and end apart: 7, of which 6 were waited for; matrix products, arithmetic and copies ran while one was open for 19% of the time, Pallas kernels for 0%

profile of v1, /device:TPU:0, one launch (start us, length us, event | category | flops | bytes accessed | tf_op | source)
XLA Modules:
  0.0 493.5 jit_solution(11711842248145956900)
XLA Ops:
  9.9 2.7 fusion.102
  16.9 24.0 %all-gather.3.cloned.1.call-done = bf16[1,2048,768]{2,1,0:T(8,128)(2,1)} async-done(((bf16[1,512,768]{2,1,0:T(8,128)(2,1)}), bf16[1,2048,768]{2,1,0:T(8,128)(2,1)}) %all-gather.3.cloned.1.call-update) | async-done | bytes 3145744 | tf_op jit(solution)/shard_map/all_gather | solution.py:96
  40.9 2.5 convert_reduce_fusion
  43.4 2.9 fusion.17
  61.8 6.3 %fusion.10 = (f32[512,3]{0,1:T(4,128)S(1)}, f32[512,3,2048]{2,0,1:T(8,128)}) fusion(pred[512,2048]{1,0:T(8,128)(4,1)S(1)} %iota_compare_fusion, bf16[1,2048,1,48]{1,3,2,0:T(8,128)(2,1)S(1)} %slice.387, bf16[1,2048,1,8]{1,3,2,0:T(8,128)(2,1)S(1)} %get-tuple-element.92, bf16[1,2048,1,8]{1,3,2,0:T(8,128)(2,1)S(1)} %get-tuple-element.91, ...), kind=kOutput, calls=%fused_computation.25 | convolution fusion | flops 412875264 | bytes 14096384 | tf_op jit(solution)/shard_map/sqhd,skd->sqhk/dot_general | solution.py:116
  70.7 6.9 %fusion = f32[512,3]{0,1:T(4,128)S(1)} fusion(f32[512,3,2048]{2,0,1:T(8,128)} %get-tuple-element.109, f32[512,3]{0,1:T(4,128)S(1)} %get-tuple-element.108, pred[512,2048]{1,0:T(8,128)(4,1)S(1)} %iota_compare_fusion), kind=kLoop, calls=%fused_computation.6 | loop fusion | flops 12581376 | bytes 13643776 | tf_op jit(solution)/shard_map/reduce_sum | solution.py:135
  78.8 3.1 fusion.194
  82.4 2.9 fusion.193
  86.4 4.8 fusion.192
  91.3 3.1 fusion.71
  94.5 7.3 %fusion.80 = f32[1,2048,64]{1,2,0:T(8,128)} fusion(f32[512,3,2048]{2,0,1:T(8,128)} %get-tuple-element.109, f32[512,3]{0,1:T(4,128)S(1)} %copy-done.49, pred[512,2048]{1,0:T(8,128)(4,1)S(1)} %iota_compare_fusion, bf16[1,2048,3,64]{1,3,2,0:T(8,128)(2,1)S(1)} %bitcast.290), kind=kOutput, calls=%fused_computation.113 | convolution fusion | flops 415236096 | bytes 14360576 | tf_op jit(solution)/shard_map/sqhk,sqhd->skd/dot_general | solution.py:206
  104.6 4.6 multiply_convert_fusion
  123.4 2.5 multiply_convert_fusion.1
  130.3 17.6 %fusion.20 = (bf16[2048,768]{1,0:T(8,128)(2,1)}, f32[2048,768]{1,0:T(8,128)S(1)}) fusion(bf16[768,768]{1,0:T(8,128)(2,1)S(1)} %copy-done, bf16[1,2048,768]{2,1,0:T(8,128)(2,1)S(1)} %copy-done.3, f32[768]{0:T(1024)S(1)} %copy-done.58, f32[768]{0:T(1024)S(1)} %copy-done.54, f32[2048]{0:T(1024)S(1)} %copy-done.39, f32[2048]{0:T(1024)S(1)} %broadcast_multiply_fusion.1), kind=kOutput, calls=%fused_computation.35 | convolution fusion | flops 2527592448 | bytes 13785088 | tf_op jit(solution)/shard_map/dot_general | solution.py:149
  147.9 5.2 %fusion.26 = bf16[2048,768]{1,0:T(8,128)(2,1)S(1)} fusion(f32[2048,768]{1,0:T(8,128)S(1)} %get-tuple-element.112, bf16[768,768]{1,0:T(8,128)(2,1)S(1)} %copy-done.57, bf16[1,2048,768]{2,1,0:T(8,128)(2,1)S(1)} %copy-done.55), kind=kOutput, calls=%fused_computation.41 | convolution fusion | flops 2431647744 | bytes 13762560 | tf_op jit(solution)/shard_map/dot_general | solution.py:63
  153.1 2.7 fusion.197
  159.0 3.0 fusion.15
  162.0 2.8 fusion.188
  166.0 7.1 %convolution_convert_fusion = bf16[768,768]{1,0:T(8,128)(2,1)} fusion(bf16[2048,768]{1,0:T(8,128)(2,1)} %copy-done.60, bf16[1,2048,768]{2,1,0:T(8,128)(2,1)} %all-gather.3.cloned.1.call-done, f32[768]{0:T(1024)S(1)} %copy-done.58, f32[768]{0:T(1024)S(1)} %copy-done.54, f32[2048]{0:T(1024)S(1)} %copy-done.39, f32[2048]{0:T(1024)S(1)} %broadcast_multiply_fusion.1), kind=kOutput, calls=%fused_computation.143 | convolution fusion | flops 2425946112 | bytes 7493632 | tf_op jit(solution)/shard_map/dot_general | solution.py:57
  173.1 3.7 fusion.104
  176.8 21.5 %all-reduce.6.cloned.1.call-done = f32[792,128]{1,0:T(8,128)} async-done(((f32[792,128]{1,0:T(8,128)}), f32[792,128]{1,0:T(8,128)}) %all-reduce.6.cloned.1.call-update) | async-done | bytes 405520 | tf_op jit(solution)/shard_map/psum | solution.py:12
  198.4 3.4 fusion.107
  201.8 3.4 fusion.110
  206.1 4.9 fusion.195
  211.0 2.7 fusion.65
  214.3 59.5 %all-reduce.8.cloned.1.call-done = f32[792,128]{1,0:T(8,128)} async-done(((f32[792,128]{1,0:T(8,128)}), f32[792,128]{1,0:T(8,128)}) %all-reduce.8.cloned.1.call-update) | async-done | bytes 405520 | tf_op jit(solution)/shard_map/psum | solution.py:13
  277.0 125.7 %all-reduce.10.cloned.1.call-done = (bf16[768,192]{0,1:T(8,128)(2,1)}, bf16[192,768]{1,0:T(8,128)(2,1)}, bf16[768,768]{1,0:T(8,128)(2,1)}, bf16[768,768]{1,0:T(8,128)(2,1)}) async-done(((bf16[768,192]{0,1:T(8,128)(2,1)}, bf16[192,768]{1,0:T(8,128)(2,1)}, bf16[768,768]{1,0:T(8,128)(2,1)}, bf16[768,768]{1,0:T(8,128)(2,1)}), (bf16[768,192]{0,1:T(8,128)(2,1)}, bf16[192,768]{1,0:T(8,128)(2,1)}, ...) | async-done | bytes 2949136 | tf_op jit(solution)/shard_map/psum | solution.py:246
  406.4 2.8 convert_element_type.267
  409.2 2.9 convert_element_type.269
  412.1 30.0 %reduce-scatter.5.cloned.1.call-done = bf16[1,512,768]{2,1,0:T(8,128)(2,1)} async-done(((bf16[1,2048,768]{2,1,0:T(8,128)(2,1)}), bf16[1,512,768]{2,1,0:T(8,128)(2,1)}) %reduce-scatter.5.cloned.1.call-update) | async-done | bytes 786448 | tf_op jit(solution)/shard_map/reduce_scatter | solution.py:236
  444.0 38.6 %reduce-scatter.3.cloned.1.call-done = bf16[1,512,768]{2,1,0:T(8,128)(2,1)} async-done(((bf16[1,2048,768]{2,1,0:T(8,128)(2,1)}), bf16[1,512,768]{2,1,0:T(8,128)(2,1)}) %reduce-scatter.3.cloned.1.call-update) | async-done | bytes 786448 | tf_op jit(solution)/shard_map/reduce_scatter | solution.py:152
  482.7 3.7 fusion.93
  (254 shorter events, 62.3 us)
Async XLA Ops:
  7.2 122.3 %copy-start = (bf16[768,768]{1,0:T(8,128)(2,1)S(1)}, bf16[768,768]{1,0:T(8,128)(2,1)}, u32[]{:S(2)}) copy-start(bf16[768,768]{1,0:T(8,128)(2,1)} %param.30) | copy-start | bytes 3538948
  7.2 39.8 %copy-start.45 = (f32[768]{0:T(1024)S(1)}, f32[768]{0:T(1024)}, u32[]{:S(2)}) copy-start(f32[768]{0:T(1024)} %param.32) | copy-start | bytes 9220
  7.2 39.8 %copy-start.53 = (f32[768]{0:T(1024)S(1)}, f32[768]{0:T(1024)}, u32[]{:S(2)}) copy-start(f32[768]{0:T(1024)} %param.33) | copy-start | bytes 9220
  7.2 33.7 %all-gather.3.cloned.1.call-start = ((), (), s32[]{:S(2)}) async-start(), calls=%async_computation.2 | async-start | bytes 3932160 | tf_op jit(solution)/shard_map/all_gather | solution.py:96
  7.9 83.3 %all-gather.5.cloned.1.call-start = ((), (), s32[]{:S(2)}) async-start(), calls=%async_computation.4 | async-start | bytes 3932160 | tf_op jit(solution)/shard_map/all_gather | solution.py:97
  12.6 185.6 %all-reduce.6.cloned.1.call-start = ((), (), s32[]{:S(2)}) async-start(), calls=%async_computation.6 | async-start | bytes 811008 | tf_op jit(solution)/shard_map/psum | solution.py:12
  12.7 28.2 %copy-start.50 = (f32[8]{0:T(128)}, f32[8]{0:T(128)S(1)}, u32[]{:S(2)}) copy-start(f32[8]{0:T(128)S(1)} %multiply_power_fusion) | copy-start | bytes 100
  16.9 35.3 %copy-start.17 = (f32[2048,8]{0,1:T(8,128)}, f32[2048,8]{0,1:T(8,128)S(1)}, u32[]{:S(2)}) copy-start(f32[2048,8]{0,1:T(8,128)S(1)} %get-tuple-element.99) | copy-start | bytes 196612
  16.9 31.6 %copy-start.19 = (bf16[768,128]{1,0:T(8,128)(2,1)S(1)}, bf16[768,128]{1,0:T(8,128)(2,1)}, u32[]{:S(2)}) copy-start(bf16[768,128]{1,0:T(8,128)(2,1)} %param.28) | copy-start | bytes 589828
  50.9 10.9 %copy-start.24 = (bf16[1,2048,1,8]{1,3,2,0:T(8,128)(2,1)}, bf16[1,2048,1,8]{1,3,2,0:T(8,128)(2,1)S(1)}, u32[]{:S(2)}) copy-start(bf16[1,2048,1,8]{1,3,2,0:T(8,128)(2,1)S(1)} %get-tuple-element.91) | copy-start | bytes 98308
  50.9 10.9 %copy-start.26 = (bf16[1,2048,1,8]{1,3,2,0:T(8,128)(2,1)}, bf16[1,2048,1,8]{1,3,2,0:T(8,128)(2,1)S(1)}, u32[]{:S(2)}) copy-start(bf16[1,2048,1,8]{1,3,2,0:T(8,128)(2,1)S(1)} %get-tuple-element.92) | copy-start | bytes 98308
  50.9 10.9 %copy-start.11 = (bf16[1,2048,1,48]{1,3,2,0:T(8,128)(2,1)}, bf16[1,2048,1,48]{1,3,2,0:T(8,128)(2,1)S(1)}, u32[]{:S(2)}) copy-start(bf16[1,2048,1,48]{1,3,2,0:T(8,128)(2,1)S(1)} %slice.387) | copy-start | bytes 589828
  57.1 21.6 %copy-start.9 = (f32[512,3,1024]{2,0,1:T(8,128)}, f32[512,3,1024]{2,0,1:T(8,128)S(1)}, u32[]{:S(2)}) copy-start(f32[512,3,1024]{2,0,1:T(8,128)S(1)} %get-tuple-element.105) | copy-start | bytes 18874372
  61.8 7.5 %copy-start.1 = (f32[512,3,1536]{2,0,1:T(8,128)}, f32[512,3,1536]{2,0,1:T(8,128)S(1)}, u32[]{:S(2)}) copy-start(f32[512,3,1536]{2,0,1:T(8,128)S(1)} %get-tuple-element.107) | copy-start | bytes 28311556
  70.7 8.1 %copy-start.15 = (bf16[1,2048,128]{1,2,0:T(8,128)(2,1)S(1)}, bf16[1,2048,128]{1,2,0:T(8,128)(2,1)}, u32[]{:S(2)}) copy-start(bf16[1,2048,128]{1,2,0:T(8,128)(2,1)} %get-tuple-element.102) | copy-start | bytes 1572868
  70.7 11.2 %slice-start = ((s8[9437184]{0:T(1024)(128)(4,1)}), s8[1048576]{0:T(1024)(128)(4,1)S(1)}, s32[]{:S(2)}) async-start(s8[9437184]{0:T(1024)(128)(4,1)} %bitcast.278), calls=%async_computation.9 | async-start | bytes 2097152
  94.4 7.4 %copy-start.7 = (f32[512,3,512]{0,2,1:T(8,128)S(1)}, f32[512,3,512]{0,2,1:T(8,128)}, u32[]{:S(2)}) copy-start(f32[512,3,512]{0,2,1:T(8,128)} %copy-done.6) | copy-start | bytes 9437188
  94.4 7.4 %copy-start.16 = (bf16[1,2048,128]{1,2,0:T(8,128)(2,1)S(1)}, bf16[1,2048,128]{1,2,0:T(8,128)(2,1)}, u32[]{:S(2)}) copy-start(bf16[1,2048,128]{1,2,0:T(8,128)(2,1)} %get-tuple-element.102) | copy-start | bytes 1572868
  94.4 7.4 %copy-start.42 = (f32[512,3]{0,1:T(4,128)S(1)}, f32[512,3]{0,1:T(4,128)}, u32[]{:S(2)}) copy-start(f32[512,3]{0,1:T(4,128)} %copy-done.41) | copy-start | bytes 18436
  94.4 9.4 %slice-start.9 = ((s8[12582912]{0:T(1024)(128)(4,1)}), s8[4194304]{0:T(1024)(128)(4,1)S(1)}, s32[]{:S(2)}) async-start(s8[12582912]{0:T(1024)(128)(4,1)} %bitcast.284), calls=%async_computation.18 | async-start | bytes 8388608
  94.4 9.4 %slice-start.10 = ((s8[12582912]{0:T(1024)(128)(4,1)}), s8[4194304]{0:T(1024)(128)(4,1)S(1)}, s32[]{:S(2)}) async-start(s8[12582912]{0:T(1024)(128)(4,1)} %bitcast.284), calls=%async_computation.19 | async-start | bytes 8388608
  130.3 17.6 %copy-start.55 = (bf16[1,2048,768]{2,1,0:T(8,128)(2,1)S(1)}, bf16[1,2048,768]{2,1,0:T(8,128)(2,1)}, u32[]{:S(2)}) copy-start(bf16[1,2048,768]{2,1,0:T(8,128)(2,1)} %all-gather.5.cloned.1.call-done) | copy-start | bytes 9437188
  130.3 17.6 %copy-start.57 = (bf16[768,768]{1,0:T(8,128)(2,1)S(1)}, bf16[768,768]{1,0:T(8,128)(2,1)}, u32[]{:S(2)}) copy-start(bf16[768,768]{1,0:T(8,128)(2,1)} %param.31) | copy-start | bytes 3538948
  165.7 108.2 %all-reduce.8.cloned.1.call-start = ((), (), s32[]{:S(2)}) async-start(), calls=%async_computation.7 | async-start | bytes 811008 | tf_op jit(solution)/shard_map/psum | solution.py:13
  173.1 28.6 %copy-start.33 = (bf16[512,3,64]{0,2,1:T(8,128)(2,1)S(1)}, bf16[512,3,64]{0,2,1:T(8,128)(2,1)}, u32[]{:S(2)}) copy-start(bf16[512,3,64]{0,2,1:T(8,128)(2,1)} %get-tuple-element.117) | copy-start | bytes 589828
  173.1 28.6 %copy-start.34 = (bf16[512,3,64]{0,2,1:T(8,128)(2,1)S(1)}, bf16[512,3,64]{0,2,1:T(8,128)(2,1)}, u32[]{:S(2)}) copy-start(bf16[512,3,64]{0,2,1:T(8,128)(2,1)} %get-tuple-element.115) | copy-start | bytes 589828
  173.1 28.6 %copy-start.35 = (bf16[512,3,64]{0,2,1:T(8,128)(2,1)S(1)}, bf16[512,3,64]{0,2,1:T(8,128)(2,1)}, u32[]{:S(2)}) copy-start(bf16[512,3,64]{0,2,1:T(8,128)(2,1)} %get-tuple-element.113) | copy-start | bytes 589828
  173.1 28.6 %copy-start.36 = (bf16[512,3,64]{0,2,1:T(8,128)(2,1)S(1)}, bf16[512,3,64]{0,2,1:T(8,128)(2,1)}, u32[]{:S(2)}) copy-start(bf16[512,3,64]{0,2,1:T(8,128)(2,1)} %get-tuple-element.110) | copy-start | bytes 589828
  198.3 204.4 %all-reduce.10.cloned.1.call-start = ((), (), s32[]{:S(2)}) async-start(), calls=%async_computation.8 | async-start | bytes 5898240 | tf_op jit(solution)/shard_map/psum | solution.py:246
  205.2 236.9 %reduce-scatter.5.cloned.1.call-start = ((), (), s32[]{:S(2)}) async-start(), calls=%async_computation.5 | async-start | bytes 3932160 | tf_op jit(solution)/shard_map/reduce_scatter | solution.py:236
  205.8 276.9 %reduce-scatter.3.cloned.1.call-start = ((), (), s32[]{:S(2)}) async-start(), calls=%async_computation.3 | async-start | bytes 3932160 | tf_op jit(solution)/shard_map/reduce_scatter | solution.py:152
  213.8 268.9 %copy-start.10 = (bf16[1,512,768]{2,1,0:T(8,128)(2,1)S(1)}, bf16[1,512,768]{2,1,0:T(8,128)(2,1)}, u32[]{:S(2)}) copy-start(bf16[1,512,768]{2,1,0:T(8,128)(2,1)} %param.24) | copy-start | bytes 2359300
  (53 other events, 196.7 us)
Sparse Core Ops, SparseCore 0:
  9.6 31.2 all-gather.2
  43.0 28.5 all-gather.4
  165.8 32.4 all-reduce.5
  201.9 71.9 all-reduce.7
  278.4 124.3 all-reduce.9
  405.3 36.7 reduce-scatter.4
  444.7 37.9 reduce-scatter.2
